TPU v7x, 256 devices: a whole 4x4x8 slice. The times are simulated.
256 devices in a mesh: trow: 32 (over z, x), tcol: 8 (over y, core).
Axes of the slice: x: 4, y: 4, z: 8, core: 2. Of those that a mesh axis runs over, the one named last changes fastest.
Arguments:
- query: bfloat16 [64, 512, 1152], P('trow', 'tcol'), may hold values from -64 to 64
- key: bfloat16 [64, 512, 1152], P('trow', 'tcol'), may hold values from -6 to 6
- value: bfloat16 [64, 512, 1152], P('trow', 'tcol'), may hold values from -6 to 6
- control: bfloat16 [64, 512, 1152], P('trow', 'tcol'), may hold values from -6 to 6
- kernel: float32 [3, 3, 1152], replicated, may hold values from -3 to 3
- grad_out: bfloat16 [64, 512, 1152], P('trow', 'tcol'), may hold values from -96 to 96
- detail_blocks: int32 [32, 8, 8], P('trow'), may hold values from -1 to 0, as said below
Outputs:
- grad_query: bfloat16 [64, 512, 1152], P('trow', 'tcol')
- grad_key: bfloat16 [64, 512, 1152], P('trow', 'tcol')
- grad_value: bfloat16 [64, 512, 1152], P('trow', 'tcol')
- grad_control: bfloat16 [64, 512, 1152], P('trow', 'tcol')
- grad_kernel: float32 [3, 3, 1152], replicated
Inputs may be any that keep to these rules, and one draw needn't show every extreme that they name: `detail_blocks`: entry [i, j, p] is the key block of tile (i, p) that tile (i, j) also attends to, or -1 for none; entry [i, j, j] is -1; each tile names blocks of 1 to 7 other tiles, and in every tile row one tile names a block of each of the other 7 tiles.
All inputs are finite; a program needn't handle non-finite values.
Results may differ from a plain program's by a relative error of at most 0.0095.
Values may be sent and summed in bfloat16 or wider, within the bound.
A program may use at most 128 MiB of HBM per device.

v0:
```python
import math
import jax
import jax.numpy as jnp
from jax import lax
from jax.sharding import PartitionSpec as P

HEADS = 16
HEAD_DIM = 72
BLOCK = 128
NEG = -1e30


def with_halo(block, sides, width):
    for axis, dim in sides:
        count = lax.axis_size(axis)
        forward = [(i, i + 1) for i in range(count - 1)]
        backward = [(target, source) for source, target in forward]
        low = lax.ppermute(
            lax.slice_in_dim(block, block.shape[dim] - width, None, axis=dim), axis, forward
        )
        high = lax.ppermute(lax.slice_in_dim(block, 0, width, axis=dim), axis, backward)
        block = jnp.concatenate([low, block, high], axis=dim)
    return block


def from_behind(shard, axis, by):
    length = lax.axis_size(axis)
    pairs = [(i, i + by) for i in range(length) if 0 <= i + by < length]
    return lax.ppermute(shard, axis, pairs)


def conv_taps(padded, kernel, rows, cols):
    total = jnp.zeros((rows, cols, padded.shape[2]), jnp.float32)
    for row_off in range(3):
        for col_off in range(3):
            total = (
                total
                + kernel[row_off, col_off][None, None, :]
                * padded[row_off : row_off + rows, col_off : col_off + cols]
            )
    return total


def conv_back(padded, kernel, rows, cols):
    total = jnp.zeros((rows, cols, padded.shape[2]), jnp.float32)
    for row_off in range(3):
        for col_off in range(3):
            total = (
                total
                + kernel[row_off, col_off][None, None, :]
                * padded[2 - row_off : 2 - row_off + rows, 2 - col_off : 2 - col_off + cols]
            )
    return total


def attend_group(queries, grads, keys, values, key_live):
    inv_root = HEAD_DIM ** (-0.5)
    scores = (
        jnp.einsum("qhd,khd->hqk", queries, keys, preferred_element_type=jnp.float32) * inv_root
    )
    scores = jnp.where(key_live[None, None, :], scores, NEG)
    row_top = jnp.max(scores, axis=2, keepdims=True)
    raised = jnp.exp(scores - row_top)
    weights = raised / jnp.sum(raised, axis=2, keepdims=True)
    weights_bf = weights.astype(jnp.bfloat16)
    attn_out = jnp.einsum("hqk,khd->qhd", weights_bf, values, preferred_element_type=jnp.float32)
    row_delta = jnp.sum(grads.astype(jnp.float32) * attn_out, axis=2)
    grad_weights = jnp.einsum("qhd,khd->hqk", grads, values, preferred_element_type=jnp.float32)
    grad_scores = weights * (grad_weights - jnp.transpose(row_delta)[:, :, None])
    grad_scores_bf = grad_scores.astype(jnp.bfloat16)
    grad_q = (
        jnp.einsum("hqk,khd->qhd", grad_scores_bf, keys, preferred_element_type=jnp.float32)
        * inv_root
    )
    grad_k = (
        jnp.einsum("hqk,qhd->khd", grad_scores_bf, queries, preferred_element_type=jnp.float32)
        * inv_root
    )
    grad_v = jnp.einsum("hqk,qhd->khd", weights_bf, grads, preferred_element_type=jnp.float32)
    return (grad_q, grad_k, grad_v)


def per_device(query, key, value, control, kernel, grad_out, detail_blocks):
    tile_rows, tile_column_count, channels = query.shape
    tile_tokens = tile_rows * tile_column_count
    tile_blocks = tile_tokens // BLOCK
    row_count = lax.axis_size("trow")
    col_count = lax.axis_size("tcol")
    my_row = lax.axis_index("trow")
    my_col = lax.axis_index("tcol")
    control_ext = with_halo(control, (("trow", 0), ("tcol", 1)), 1).astype(jnp.float32)
    v_ctrl = (
        value.astype(jnp.float32) + conv_taps(control_ext, kernel, tile_rows, tile_column_count)
    ).astype(jnp.bfloat16)
    query_flat = query.reshape(tile_tokens, channels)
    key_flat = key.reshape(tile_tokens, channels)
    value_flat = v_ctrl.reshape(tile_tokens, channels)
    grad_flat = grad_out.reshape(tile_tokens, channels)
    above = from_behind((key_flat, value_flat), "trow", 1)
    below = from_behind((key_flat, value_flat), "trow", -1)
    pattern = detail_blocks[0]
    wanted = lax.dynamic_index_in_dim(pattern, my_col, 0, keepdims=False)
    asked = lax.dynamic_index_in_dim(pattern, my_col, 1, keepdims=False)
    slot_ids = jnp.arange(col_count - 1, dtype=jnp.int32)
    others = slot_ids + (slot_ids >= my_col).astype(jnp.int32)
    wanted_others = wanted[others]
    row_keys, row_values = (
        lax.all_gather(key_flat, "tcol", axis=0, tiled=True),
        lax.all_gather(value_flat, "tcol", axis=0, tiled=True),
    )
    picked = others * tile_blocks + jnp.maximum(wanted_others, 0)
    detail_keys = row_keys.reshape(col_count * tile_blocks, BLOCK, channels)[picked]
    detail_values = row_values.reshape(col_count * tile_blocks, BLOCK, channels)[picked]
    detail_count = (col_count - 1) * BLOCK
    all_keys = jnp.concatenate(
        [key_flat, above[0], below[0], detail_keys.reshape(detail_count, channels)], axis=0
    )
    all_values = jnp.concatenate(
        [value_flat, above[1], below[1], detail_values.reshape(detail_count, channels)], axis=0
    )
    key_live = jnp.concatenate(
        [
            jnp.ones((tile_tokens,), bool),
            jnp.full((tile_tokens,), my_row >= 1),
            jnp.full((tile_tokens,), my_row + 1 < row_count),
            jnp.repeat(wanted_others >= 0, BLOCK),
        ],
        axis=0,
    )
    head_group = math.gcd(HEADS, 4)
    col_span = head_group * HEAD_DIM
    query_parts = []
    key_parts = []
    value_parts = []
    for group_index in range(HEADS // head_group):
        low = group_index * col_span
        high = low + col_span
        grad_q, grad_k, grad_v = attend_group(
            query_flat[:, low:high].reshape(-1, head_group, HEAD_DIM),
            grad_flat[:, low:high].reshape(-1, head_group, HEAD_DIM),
            all_keys[:, low:high].reshape(-1, head_group, HEAD_DIM),
            all_values[:, low:high].reshape(-1, head_group, HEAD_DIM),
            key_live,
        )
        query_parts.append(grad_q.reshape(-1, col_span))
        key_parts.append(grad_k.reshape(-1, col_span))
        value_parts.append(grad_v.reshape(-1, col_span))
    query_gradient_total = jnp.concatenate(query_parts, axis=1)
    grad_k_all = jnp.concatenate(key_parts, axis=1)
    grad_v_all = jnp.concatenate(value_parts, axis=1)
    up_terms = from_behind(
        (grad_k_all[tile_tokens : 2 * tile_tokens], grad_v_all[tile_tokens : 2 * tile_tokens]),
        "trow",
        -1,
    )
    down_terms = from_behind(
        (
            grad_k_all[2 * tile_tokens : 3 * tile_tokens],
            grad_v_all[2 * tile_tokens : 3 * tile_tokens],
        ),
        "trow",
        1,
    )
    slot_k = (
        grad_k_all[3 * tile_tokens :].reshape(col_count - 1, BLOCK, channels).astype(jnp.bfloat16)
    )
    slot_v = (
        grad_v_all[3 * tile_tokens :].reshape(col_count - 1, BLOCK, channels).astype(jnp.bfloat16)
    )
    detail_k = jnp.zeros((col_count, BLOCK, channels), jnp.bfloat16).at[others].set(slot_k)
    detail_v = jnp.zeros((col_count, BLOCK, channels), jnp.bfloat16).at[others].set(slot_v)
    returned_keys, returned_values = (
        lax.all_to_all(detail_k, "tcol", split_axis=0, concat_axis=0, tiled=True),
        lax.all_to_all(detail_v, "tcol", split_axis=0, concat_axis=0, tiled=True),
    )
    tile_owner_lookup = (
        asked[None, :] == jnp.arange(tile_blocks, dtype=jnp.int32)[:, None]
    ).astype(jnp.bfloat16)
    served_keys = jnp.einsum(
        "ev,vsw->esw", tile_owner_lookup, returned_keys, preferred_element_type=jnp.float32
    ).reshape(tile_tokens, channels)
    served_values = jnp.einsum(
        "ev,vsw->esw", tile_owner_lookup, returned_values, preferred_element_type=jnp.float32
    ).reshape(tile_tokens, channels)
    grad_key = (grad_k_all[:tile_tokens] + up_terms[0] + down_terms[0] + served_keys).astype(
        jnp.bfloat16
    )
    grad_value = (grad_v_all[:tile_tokens] + up_terms[1] + down_terms[1] + served_values).astype(
        jnp.bfloat16
    )
    grad_value_img = grad_value.reshape(tile_rows, tile_column_count, channels)
    value_ext = with_halo(grad_value_img, (("trow", 0), ("tcol", 1)), 1).astype(jnp.float32)
    grad_control = conv_back(value_ext, kernel, tile_rows, tile_column_count).astype(jnp.bfloat16)
    grad_value_f = grad_value_img.astype(jnp.float32)
    kernel_rows = []
    for row_off in range(3):
        kernel_cols = []
        for col_off in range(3):
            kernel_cols.append(
                jnp.sum(
                    control_ext[
                        row_off : row_off + tile_rows, col_off : col_off + tile_column_count
                    ]
                    * grad_value_f,
                    axis=(0, 1),
                )
            )
        kernel_rows.append(jnp.stack(kernel_cols, axis=0))
    grad_kernel = lax.psum(jnp.stack(kernel_rows, axis=0), ("trow", "tcol"))
    grad_query = query_gradient_total.astype(jnp.bfloat16).reshape(
        tile_rows, tile_column_count, channels
    )
    return (
        grad_query,
        grad_key.reshape(tile_rows, tile_column_count, channels),
        grad_value_img,
        grad_control,
        grad_kernel,
    )


def solution(mesh):
    return jax.shard_map(
        per_device,
        mesh=mesh,
        in_specs=(
            P("trow", "tcol", None),
            P("trow", "tcol", None),
            P("trow", "tcol", None),
            P("trow", "tcol", None),
            P(),
            P("trow", "tcol", None),
            P("trow", None, None),
        ),
        out_specs=(
            P("trow", "tcol", None),
            P("trow", "tcol", None),
            P("trow", "tcol", None),
            P("trow", "tcol", None),
            P(),
        ),
        check_vma=False,
    )
```

profile of v0, /device:TPU:1, one launch (start us, length us, event | category | flops | bytes accessed | tf_op | source)
XLA Modules:
  0.0 365.8 jit_solution(7707213717412692028)
XLA Ops:
  9.3 5.3 %collective-permute-start = (bf16[128,1152]{1,0:T(8,128)(2,1)}, bf16[128,1152]{1,0:T(8,128)(2,1)}, u32[]{:S(2)}, u32[]{:S(2)}) collective-permute-start(bf16[128,1152]{1,0:T(8,128)(2,1)} %bitcast.267), channel_id=1, source_target_pairs={{0,8},{8,16},{16,24},{24,32},{32,40},{40,48},{48,56},{56,64},{64,7... | collective-permute-start | bytes 884744 | tf_op jit(solution)/shard_map/ppermute | solution.py:29
  15.6 2.6 collective-permute-start.2
  24.2 4.9 %collective-permute-start.5 = (bf16[4,1,1152]{2,1,0:T(2,128)(2,1)S(1)}, bf16[4,1,1152]{2,1,0:T(2,128)(2,1)S(1)}, u32[]{:S(2)}, u32[]{:S(2)}) collective-permute-start(bf16[4,1,1152]{2,1,0:T(2,128)(2,1)S(1)} %get-tuple-element.43), channel_id=1, source_target_pairs={{1,0},{2,1},{3,2},{4,3},{5,4},{6,5},{7,6},{9,8},{10,9},{11,10},{12... | collective-permute-start | bytes 27656 | tf_op jit(solution)/shard_map/ppermute | solution.py:21
  29.1 2.8 collective-permute-start.4
  40.7 5.8 %collective-permute-start.6 = (bf16[128,1152]{1,0:T(8,128)(2,1)}, bf16[128,1152]{1,0:T(8,128)(2,1)}, u32[]{:S(2)}, u32[]{:S(2)}) collective-permute-start(bf16[128,1152]{1,0:T(8,128)(2,1)} %bitcast.12), channel_id=1, source_target_pairs={{0,8},{8,16},{16,24},{24,32},{32,40},{40,48},{48,56},{56,64},{64,7... | collective-permute-start | bytes 884744 | tf_op jit(solution)/shard_map/ppermute | solution.py:29
  46.5 2.7 gather_fusion.1
  50.6 3.0 fusion.101
  55.9 4.0 %fusion.108 = (f32[4,128]{1,0:T(4,128)S(1)}, f32[4,128,1280]{1,2,0:T(8,128)}) fusion(bf16[1280,4,72]{0,2,1:T(8,128)(2,1)} %bitcast.257, bf16[128,4,72]{0,2,1:T(8,128)(2,1)S(1)} %bitcast.287, pred[1280]{0:T(1024)(128)(4,1)S(1)} %copy-done.47), kind=kOutput, calls=%fused_computation.197 | convolution fusion | flops 96994560 | bytes 3435776 | tf_op jit(solution)/shard_map/sub | solution.py:63
  59.9 2.7 fusion.109
  70.3 3.0 copy.87
  78.5 2.7 copy.88
  81.3 3.6 fusion.107
  90.0 2.8 copy.89
  92.9 3.5 fusion.106
  101.5 2.8 copy.90
  104.3 8.9 %concatenate.51 = f32[1280,1152]{1,0:T(8,128)} concatenate(f32[1280,288]{1,0:T(8,128)} %copy.87, f32[1280,288]{1,0:T(8,128)} %copy.88, f32[1280,288]{1,0:T(8,128)} %copy.89, f32[1280,288]{1,0:T(8,128)} %copy.90), dimensions={1} | concatenate | bytes 11796480 | tf_op jit(solution)/shard_map/concatenate | solution.py:150
  113.1 3.7 %slice.404 = bf16[896,1152]{1,0:T(8,128)(2,1)} slice(f32[1280,1152]{1,0:T(8,128)} %concatenate.51), slice={[384:1280], [0:1152]} | slice | bytes 4128768 | tf_op jit(solution)/shard_map/slice | solution.py:168
  116.8 2.4 fusion.98
  119.2 3.7 %collective-permute-start.11 = (f32[128,1152]{1,0:T(8,128)}, f32[128,1152]{1,0:T(8,128)}, u32[]{:S(2)}, u32[]{:S(2)}) collective-permute-start(f32[128,1152]{1,0:T(8,128)} %get-tuple-element.29), channel_id=1, source_target_pairs={{0,8},{8,16},{16,24},{24,32},{32,40},{40,48},{48,56},{56,64},{64,7... | collective-permute-start | bytes 1769480 | tf_op jit(solution)/shard_map/ppermute | solution.py:29
  125.9 5.8 %scatter_fusion.1 = bf16[8,128,1152]{2,1,0:T(8,128)(2,1)} fusion(bf16[8,128,1152]{2,1,0:T(8,128)(2,1)} %broadcast.125.clone.1, s32[7]{0:T(128)S(1)} %copy-done.44, bf16[7,128,1152]{2,1,0:T(8,128)(2,1)} %bitcast.233), kind=kCustom, calls=%fused_computation.4 | custom fusion | bytes 6193180 | tf_op jit(solution)/shard_map/scatter | solution.py:171
  131.7 4.7 %all-to-all-start.1 = ((bf16[8,128,1152]{2,1,0:T(8,128)(2,1)}), bf16[8,128,1152]{2,1,0:T(8,128)(2,1)}, u32[]{:S(2)}, u32[]{:S(2)}) async-start(bf16[8,128,1152]{2,1,0:T(8,128)(2,1)} %scatter_fusion.1), calls=%async_computation.1 | async-start | bytes 4718592 | tf_op jit(solution)/shard_map/all_to_all | solution.py:174
  136.4 3.9 %gather_fusion.2 = bf16[7,128,1152]{2,1,0:T(8,128)(2,1)} fusion(bf16[8,128,1152]{2,1,0:T(8,128)(2,1)} %bitcast.264, s32[1024]{0:T(1024)} %pad_clamp_fusion), kind=kCustom, calls=%fused_computation.2 | custom fusion | bytes 4128796 | tf_op jit(solution)/shard_map/gather | solution.py:113
  142.4 3.6 fusion.100
  149.2 2.5 fusion.28
  157.1 2.5 fusion.29
  165.1 2.5 fusion.30
  171.6 2.5 fusion.31
  176.7 6.4 %pad_maximum_fusion.2 = bf16[2,64,1152]{1,0,2:T(2,128)(2,1)S(1)} fusion(bf16[2,64,288]{1,0,2:T(2,128)(2,1)S(1)} %concatenate.48, bf16[2,64,288]{1,0,2:T(2,128)(2,1)S(1)} %concatenate.47, bf16[2,64,288]{1,0,2:T(2,128)(2,1)} %concatenate.46, bf16[2,64,288]{1,0,2:T(2,128)(2,1)} %concatenate.45), kind=kLoop, calls=%fused_computation.135 | loop fusion | flops 442368 | bytes 589824 | tf_op jit(solution)/shard_map/concatenate | solution.py:148
  184.5 2.9 convolution_multiply_fusion.7
  189.3 3.4 convolution_multiply_fusion.6
  192.7 2.8 copy.80
  195.5 3.3 convolution_multiply_fusion.5
  198.8 2.8 copy.81
  201.6 3.4 convolution_multiply_fusion.4
  205.0 2.7 copy.82
  207.7 8.5 %concatenate.50 = f32[1280,1152]{1,0:T(8,128)} concatenate(f32[1280,288]{1,0:T(8,128)S(1)} %copy.79, f32[1280,288]{1,0:T(8,128)} %copy.80, f32[1280,288]{1,0:T(8,128)} %copy.81, f32[1280,288]{1,0:T(8,128)} %copy.82), dimensions={1} | concatenate | bytes 11796480 | tf_op jit(solution)/shard_map/concatenate | solution.py:149
  216.3 2.4 slice.405
  218.6 2.3 fusion.99
  221.0 5.1 %collective-permute-start.9 = (f32[128,1152]{1,0:T(8,128)}, f32[128,1152]{1,0:T(8,128)}, u32[]{:S(2)}, u32[]{:S(2)}) collective-permute-start(f32[128,1152]{1,0:T(8,128)} %get-tuple-element.31), channel_id=1, source_target_pairs={{0,8},{8,16},{16,24},{24,32},{32,40},{40,48},{48,56},{56,64},{64,7... | collective-permute-start | bytes 1769480 | tf_op jit(solution)/shard_map/ppermute | solution.py:29
  229.1 5.1 %scatter_fusion = bf16[8,128,1152]{2,1,0:T(8,128)(2,1)} fusion(bf16[8,128,1152]{2,1,0:T(8,128)(2,1)} %broadcast.125.clone, s32[7]{0:T(128)S(1)} %copy-done.45, bf16[7,128,1152]{2,1,0:T(8,128)(2,1)S(1)} %bitcast.232), kind=kCustom, calls=%fused_computation.3 | custom fusion | bytes 6193180 | tf_op jit(solution)/shard_map/scatter | solution.py:170
  234.3 5.2 %all-to-all-start = ((bf16[8,128,1152]{2,1,0:T(8,128)(2,1)}), bf16[8,128,1152]{2,1,0:T(8,128)(2,1)}, u32[]{:S(2)}, u32[]{:S(2)}) async-start(bf16[8,128,1152]{2,1,0:T(8,128)(2,1)} %scatter_fusion), calls=%async_computation | async-start | bytes 4718592 | tf_op jit(solution)/shard_map/all_to_all | solution.py:173
  239.4 3.3 fusion.32
  245.6 5.6 %collective-permute-start.12 = (bf16[1,64,1152]{2,1,0:T(8,128)(2,1)S(1)}, bf16[1,64,1152]{2,1,0:T(8,128)(2,1)S(1)}, u32[]{:S(2)}, u32[]{:S(2)}) collective-permute-start(bf16[1,64,1152]{2,1,0:T(8,128)(2,1)S(1)} %get-tuple-element.44), channel_id=1, source_target_pairs={{0,8},{8,16},{16,24},{24,32},{32,40},{40,48},{48,56},{56,64},{64,7... | collective-permute-start | bytes 442376 | tf_op jit(solution)/shard_map/ppermute | solution.py:18
  252.0 94.0 %psum.7 = f32[3,3,1152]{2,1,0:T(4,128)} all-reduce(f32[3,3,1152]{2,1,0:T(4,128)S(1)} %pad_maximum_fusion.3), channel_id=1, replica_groups=mesh['trow'=32,'tcol'=8] {'trow','tcol'}, use_global_device_ids=true, to_apply=%region_23.24 | all-reduce | flops 10368 | bytes 82944 | tf_op jit(solution)/shard_map/psum | solution.py:209
  346.0 2.6 collective-permute-start.15
  348.6 3.0 collective-permute-start.14
  351.6 3.3 fusion.34
  355.0 2.3 fusion.79
  (209 shorter events, 81.1 us)
Async XLA Ops:
  7.2 16.1 %copy-start.14 = (bf16[2,64,1152]{2,1,0:T(8,128)(2,1)S(1)}, bf16[2,64,1152]{2,1,0:T(8,128)(2,1)}, u32[]{:S(2)}) copy-start(bf16[2,64,1152]{2,1,0:T(8,128)(2,1)} %param.10) | copy-start | bytes 884740
  7.2 15.1 %copy-start.17 = (bf16[2,64,1152]{2,1,0:T(8,128)(2,1)S(1)}, bf16[2,64,1152]{2,1,0:T(8,128)(2,1)}, u32[]{:S(2)}) copy-start(bf16[2,64,1152]{2,1,0:T(8,128)(2,1)} %param.7) | copy-start | bytes 884740
  7.2 15.8 %copy-start.41 = (f32[3,3,1152]{2,1,0:T(4,128)S(1)}, f32[3,3,1152]{2,1,0:T(4,128)}, u32[]{:S(2)}) copy-start(f32[3,3,1152]{2,1,0:T(4,128)} %param.11) | copy-start | bytes 124420
  7.2 39.3 %all-gather.3.cloned.1.call-start = ((), (), s32[]{:S(2)}) async-start(), calls=%async_computation.2 | async-start | bytes 2654208 | tf_op jit(solution)/shard_map/all_gather | solution.py:108
  7.9 128.5 %all-gather.5.cloned.1.call-start = ((), (), s32[]{:S(2)}) async-start(), calls=%async_computation.3 | async-start | bytes 2654208 | tf_op jit(solution)/shard_map/all_gather | solution.py:109
  8.0 41.2 %collective-permute-start.1 = (bf16[128,1152]{1,0:T(8,128)(2,1)}, bf16[128,1152]{1,0:T(8,128)(2,1)}, u32[]{:S(2)}, u32[]{:S(2)}) collective-permute-start(bf16[128,1152]{1,0:T(8,128)(2,1)} %bitcast.266), channel_id=1, source_target_pairs={{8,0},{16,8},{24,16},{32,24},{40,32},{48,40},{56,48},{64,56},{72,6... | collective-permute-start | bytes 884744 | tf_op jit(solution)/shard_map/ppermute | solution.py:29
  9.3 39.9 %collective-permute-start = (bf16[128,1152]{1,0:T(8,128)(2,1)}, bf16[128,1152]{1,0:T(8,128)(2,1)}, u32[]{:S(2)}, u32[]{:S(2)}) collective-permute-start(bf16[128,1152]{1,0:T(8,128)(2,1)} %bitcast.267), channel_id=1, source_target_pairs={{0,8},{8,16},{16,24},{24,32},{32,40},{40,48},{48,56},{56,64},{64,7... | collective-permute-start | bytes 884744 | tf_op jit(solution)/shard_map/ppermute | solution.py:29
  15.6 7.6 %collective-permute-start.2 = (bf16[1,64,1152]{2,1,0:T(8,128)(2,1)S(1)}, bf16[1,64,1152]{2,1,0:T(8,128)(2,1)S(1)}, u32[]{:S(2)}, u32[]{:S(2)}) collective-permute-start(bf16[1,64,1152]{2,1,0:T(8,128)(2,1)S(1)} %get-tuple-element.55), channel_id=1, source_target_pairs={{0,8},{8,16},{16,24},{24,32},{32,40},{40,48},{48,56},{56,64},{64,7... | collective-permute-start | bytes 442376 | tf_op jit(solution)/shard_map/ppermute | solution.py:18
  18.2 5.9 %collective-permute-start.3 = (bf16[1,64,1152]{2,1,0:T(8,128)(2,1)S(1)}, bf16[1,64,1152]{2,1,0:T(8,128)(2,1)S(1)}, u32[]{:S(2)}, u32[]{:S(2)}) collective-permute-start(bf16[1,64,1152]{2,1,0:T(8,128)(2,1)S(1)} %get-tuple-element.54), channel_id=1, source_target_pairs={{8,0},{16,8},{24,16},{32,24},{40,32},{48,40},{56,48},{64,56},{72,6... | collective-permute-start | bytes 442376 | tf_op jit(solution)/shard_map/ppermute | solution.py:21
  20.3 17.0 %copy-start.46 = (s32[1,8,8]{2,1,0:T(8,128)S(1)}, s32[1,8,8]{2,1,0:T(8,128)}, u32[]{:S(2)}) copy-start(s32[1,8,8]{2,1,0:T(8,128)} %param.13) | copy-start | bytes 772
  23.0 15.1 %copy-start.18 = (bf16[2,64,1152]{2,1,0:T(8,128)(2,1)S(1)}, bf16[2,64,1152]{2,1,0:T(8,128)(2,1)}, u32[]{:S(2)}) copy-start(bf16[2,64,1152]{2,1,0:T(8,128)(2,1)} %param.9) | copy-start | bytes 884740
  23.1 16.2 %copy-start.27 = (f32[1152]{0:T(1024)}, f32[1152]{0:T(1024)S(1)}, u32[]{:S(2)}) copy-start(f32[1152]{0:T(1024)S(1)} %get-tuple-element.21) | copy-start | bytes 13828
  23.1 16.2 %copy-start.29 = (f32[1152]{0:T(1024)}, f32[1152]{0:T(1024)S(1)}, u32[]{:S(2)}) copy-start(f32[1152]{0:T(1024)S(1)} %get-tuple-element.22) | copy-start | bytes 13828
  23.2 16.2 %copy-start.31 = (f32[1152]{0:T(1024)}, f32[1152]{0:T(1024)S(1)}, u32[]{:S(2)}) copy-start(f32[1152]{0:T(1024)S(1)} %get-tuple-element.23) | copy-start | bytes 13828
  23.2 16.2 %copy-start.33 = (f32[1152]{0:T(1024)}, f32[1152]{0:T(1024)S(1)}, u32[]{:S(2)}) copy-start(f32[1152]{0:T(1024)S(1)} %get-tuple-element.24) | copy-start | bytes 13828
  23.2 16.2 %copy-start.35 = (f32[1152]{0:T(1024)}, f32[1152]{0:T(1024)S(1)}, u32[]{:S(2)}) copy-start(f32[1152]{0:T(1024)S(1)} %get-tuple-element.25) | copy-start | bytes 13828
  23.2 16.2 %copy-start.37 = (f32[1152]{0:T(1024)}, f32[1152]{0:T(1024)S(1)}, u32[]{:S(2)}) copy-start(f32[1152]{0:T(1024)S(1)} %get-tuple-element.26) | copy-start | bytes 13828
  23.2 16.2 %copy-start.39 = (f32[1152]{0:T(1024)}, f32[1152]{0:T(1024)S(1)}, u32[]{:S(2)}) copy-start(f32[1152]{0:T(1024)S(1)} %get-tuple-element.27) | copy-start | bytes 13828
  24.2 13.7 %collective-permute-start.5 = (bf16[4,1,1152]{2,1,0:T(2,128)(2,1)S(1)}, bf16[4,1,1152]{2,1,0:T(2,128)(2,1)S(1)}, u32[]{:S(2)}, u32[]{:S(2)}) collective-permute-start(bf16[4,1,1152]{2,1,0:T(2,128)(2,1)S(1)} %get-tuple-element.43), channel_id=1, source_target_pairs={{1,0},{2,1},{3,2},{4,3},{5,4},{6,5},{7,6},{9,8},{10,9},{11,10},{12... | collective-permute-start | bytes 27656 | tf_op jit(solution)/shard_map/ppermute | solution.py:21
  29.1 8.8 %collective-permute-start.4 = (bf16[4,1,1152]{2,1,0:T(2,128)(2,1)S(1)}, bf16[4,1,1152]{2,1,0:T(2,128)(2,1)S(1)}, u32[]{:S(2)}, u32[]{:S(2)}) collective-permute-start(bf16[4,1,1152]{2,1,0:T(2,128)(2,1)S(1)} %get-tuple-element.42), channel_id=1, source_target_pairs={{0,1},{1,2},{2,3},{3,4},{4,5},{5,6},{6,7},{8,9},{9,10},{10,11},{11... | collective-permute-start | bytes 27656 | tf_op jit(solution)/shard_map/ppermute | solution.py:18
  39.4 101.0 %collective-permute-start.7 = (bf16[128,1152]{1,0:T(8,128)(2,1)}, bf16[128,1152]{1,0:T(8,128)(2,1)}, u32[]{:S(2)}, u32[]{:S(2)}) collective-permute-start(bf16[128,1152]{1,0:T(8,128)(2,1)} %bitcast.12), channel_id=1, source_target_pairs={{8,0},{16,8},{24,16},{32,24},{40,32},{48,40},{56,48},{64,56},{72,6... | collective-permute-start | bytes 884744 | tf_op jit(solution)/shard_map/ppermute | solution.py:29
  40.7 99.7 %collective-permute-start.6 = (bf16[128,1152]{1,0:T(8,128)(2,1)}, bf16[128,1152]{1,0:T(8,128)(2,1)}, u32[]{:S(2)}, u32[]{:S(2)}) collective-permute-start(bf16[128,1152]{1,0:T(8,128)(2,1)} %bitcast.12), channel_id=1, source_target_pairs={{0,8},{8,16},{16,24},{24,32},{32,40},{40,48},{48,56},{56,64},{64,7... | collective-permute-start | bytes 884744 | tf_op jit(solution)/shard_map/ppermute | solution.py:29
  55.8 4.1 %copy-start.7 = (bf16[1280,288]{0,1:T(8,128)(2,1)}, bf16[1280,288]{0,1:T(8,128)(2,1)S(1)}, u32[]{:S(2)}) copy-start(bf16[1280,288]{0,1:T(8,128)(2,1)S(1)} %copy.51) | copy-start | bytes 2211844
  55.9 4.0 %copy-start.26 = (bf16[128,288]{0,1:T(8,128)(2,1)S(1)}, bf16[128,288]{0,1:T(8,128)(2,1)}, u32[]{:S(2)}) copy-start(bf16[128,288]{0,1:T(8,128)(2,1)} %copy.112) | copy-start | bytes 221188
  70.3 11.0 %copy-start.10 = (bf16[1280,288]{0,1:T(8,128)(2,1)}, bf16[1280,288]{0,1:T(8,128)(2,1)S(1)}, u32[]{:S(2)}) copy-start(bf16[1280,288]{0,1:T(8,128)(2,1)S(1)} %copy.63) | copy-start | bytes 2211844
  84.9 3.1 copy-start.15
  90.0 2.9 copy-start.12
  96.4 3.0 copy-start.16
  116.8 9.1 %copy-start.44 = (s32[7]{0:T(128)S(1)}, s32[7]{0:T(128)}, u32[]{:S(2)}) copy-start(s32[7]{0:T(128)} %copy-done.43) | copy-start | bytes 88
  119.2 123.5 %collective-permute-start.11 = (f32[128,1152]{1,0:T(8,128)}, f32[128,1152]{1,0:T(8,128)}, u32[]{:S(2)}, u32[]{:S(2)}) collective-permute-start(f32[128,1152]{1,0:T(8,128)} %get-tuple-element.29), channel_id=1, source_target_pairs={{0,8},{8,16},{16,24},{24,32},{32,40},{40,48},{48,56},{56,64},{64,7... | collective-permute-start | bytes 1769480 | tf_op jit(solution)/shard_map/ppermute | solution.py:29
  122.9 119.8 %collective-permute-start.10 = (f32[128,1152]{1,0:T(8,128)}, f32[128,1152]{1,0:T(8,128)}, u32[]{:S(2)}, u32[]{:S(2)}) collective-permute-start(f32[128,1152]{1,0:T(8,128)} %get-tuple-element.28), channel_id=1, source_target_pairs={{8,0},{16,8},{24,16},{32,24},{40,32},{48,40},{56,48},{64,56},{72,6... | collective-permute-start | bytes 1769480 | tf_op jit(solution)/shard_map/ppermute | solution.py:29
  131.7 102.5 %all-to-all-start.1 = ((bf16[8,128,1152]{2,1,0:T(8,128)(2,1)}), bf16[8,128,1152]{2,1,0:T(8,128)(2,1)}, u32[]{:S(2)}, u32[]{:S(2)}) async-start(bf16[8,128,1152]{2,1,0:T(8,128)(2,1)} %scatter_fusion.1), calls=%async_computation.1 | async-start | bytes 4718592 | tf_op jit(solution)/shard_map/all_to_all | solution.py:174
  149.2 3.6 copy-start.13
  157.1 3.7 %copy-start.11 = (bf16[1280,288]{0,1:T(8,128)(2,1)S(1)}, bf16[1280,288]{0,1:T(8,128)(2,1)}, u32[]{:S(2)}) copy-start(bf16[1280,288]{0,1:T(8,128)(2,1)} %copy-done.10) | copy-start | bytes 2211844
  165.0 3.6 copy-start.9
  171.6 3.0 copy-start.19
  192.6 2.8 copy-start.23
  198.8 2.8 copy-start.22
  218.6 10.5 %copy-start.45 = (s32[7]{0:T(128)S(1)}, s32[7]{0:T(128)}, u32[]{:S(2)}) copy-start(s32[7]{0:T(128)} %copy-done.43) | copy-start | bytes 88
  221.0 134.0 %collective-permute-start.9 = (f32[128,1152]{1,0:T(8,128)}, f32[128,1152]{1,0:T(8,128)}, u32[]{:S(2)}, u32[]{:S(2)}) collective-permute-start(f32[128,1152]{1,0:T(8,128)} %get-tuple-element.31), channel_id=1, source_target_pairs={{0,8},{8,16},{16,24},{24,32},{32,40},{40,48},{48,56},{56,64},{64,7... | collective-permute-start | bytes 1769480 | tf_op jit(solution)/shard_map/ppermute | solution.py:29
  226.1 128.9 %collective-permute-start.8 = (f32[128,1152]{1,0:T(8,128)}, f32[128,1152]{1,0:T(8,128)}, u32[]{:S(2)}, u32[]{:S(2)}) collective-permute-start(f32[128,1152]{1,0:T(8,128)} %get-tuple-element.30), channel_id=1, source_target_pairs={{8,0},{16,8},{24,16},{32,24},{40,32},{48,40},{56,48},{64,56},{72,6... | collective-permute-start | bytes 1769480 | tf_op jit(solution)/shard_map/ppermute | solution.py:29
  234.3 5.2 %copy-start.42 = (pred[8]{0:T(512)(128)(4,1)S(1)}, pred[8]{0:T(512)(128)(4,1)}, u32[]{:S(2)}) copy-start(pred[8]{0:T(512)(128)(4,1)} %fusion.80) | copy-start | bytes 28
  234.3 117.4 %all-to-all-start = ((bf16[8,128,1152]{2,1,0:T(8,128)(2,1)}), bf16[8,128,1152]{2,1,0:T(8,128)(2,1)}, u32[]{:S(2)}, u32[]{:S(2)}) async-start(bf16[8,128,1152]{2,1,0:T(8,128)(2,1)} %scatter_fusion), calls=%async_computation | async-start | bytes 4718592 | tf_op jit(solution)/shard_map/all_to_all | solution.py:173
  244.2 113.0 %copy-start.3 = (bf16[128,1152]{1,0:T(8,128)(2,1)}, bf16[128,1152]{1,0:T(8,128)(2,1)S(1)}, u32[]{:S(2)}) copy-start(bf16[128,1152]{1,0:T(8,128)(2,1)S(1)} %fusion.76) | copy-start | bytes 884740
  244.3 101.7 %collective-permute-start.13 = (bf16[1,64,1152]{2,1,0:T(8,128)(2,1)S(1)}, bf16[1,64,1152]{2,1,0:T(8,128)(2,1)S(1)}, u32[]{:S(2)}, u32[]{:S(2)}) collective-permute-start(bf16[1,64,1152]{2,1,0:T(8,128)(2,1)S(1)} %get-tuple-element.45), channel_id=1, source_target_pairs={{8,0},{16,8},{24,16},{32,24},{40,32},{48,40},{56,48},{64,56},{72,6... | collective-permute-start | bytes 442376 | tf_op jit(solution)/shard_map/ppermute | solution.py:21
  245.6 100.4 %collective-permute-start.12 = (bf16[1,64,1152]{2,1,0:T(8,128)(2,1)S(1)}, bf16[1,64,1152]{2,1,0:T(8,128)(2,1)S(1)}, u32[]{:S(2)}, u32[]{:S(2)}) collective-permute-start(bf16[1,64,1152]{2,1,0:T(8,128)(2,1)S(1)} %get-tuple-element.44), channel_id=1, source_target_pairs={{0,8},{8,16},{16,24},{24,32},{32,40},{40,48},{48,56},{56,64},{64,7... | collective-permute-start | bytes 442376 | tf_op jit(solution)/shard_map/ppermute | solution.py:18
  346.0 11.2 %collective-permute-start.15 = (bf16[4,1,1152]{2,1,0:T(2,128)(2,1)S(1)}, bf16[4,1,1152]{2,1,0:T(2,128)(2,1)S(1)}, u32[]{:S(2)}, u32[]{:S(2)}) collective-permute-start(bf16[4,1,1152]{2,1,0:T(2,128)(2,1)S(1)} %get-tuple-element.41), channel_id=1, source_target_pairs={{1,0},{2,1},{3,2},{4,3},{5,4},{6,5},{7,6},{9,8},{10,9},{11,10},{12... | collective-permute-start | bytes 27656 | tf_op jit(solution)/shard_map/ppermute | solution.py:21
  348.6 8.6 %collective-permute-start.14 = (bf16[4,1,1152]{2,1,0:T(2,128)(2,1)S(1)}, bf16[4,1,1152]{2,1,0:T(2,128)(2,1)S(1)}, u32[]{:S(2)}, u32[]{:S(2)}) collective-permute-start(bf16[4,1,1152]{2,1,0:T(2,128)(2,1)S(1)} %get-tuple-element.40), channel_id=1, source_target_pairs={{0,1},{1,2},{2,3},{3,4},{4,5},{5,6},{6,7},{8,9},{9,10},{10,11},{11... | collective-permute-start | bytes 27656 | tf_op jit(solution)/shard_map/ppermute | solution.py:18
  (20 other events, 36.6 us)
Sparse Core Ops, SparseCore 0:
  9.8 32.3 all-gather.2
  46.6 34.6 all-gather.4
where the time goes:
time: 373 us; the launch traced here: 366 us
  local copies, waits for them, and re-layouts  108 us (29%)
  blocking collectives  94 us (25%)
  matrix products  60.8 us (16%)
  starting transfers between devices  59 us (16%)
  other arithmetic  26.9 us (7%)
  between operations  15.3 us (4%)
    psum x1, blocking collectives, per_device(): grad_kernel = lax.psum(jnp.stack(kernel_rows, axis=0), ('trow', 'tcol'))  94 us
    ppermute x8, starting transfers between devices, from_behind(): return lax.ppermute(shard, axis, pairs)  25 us
    ppermute x4, starting transfers between devices, with_halo(): lax.ppermute(lax.slice_in_dim(block, block.shape[dim] - width, None, axis...  14 us
    sub x4, matrix products, attend_group(): raised = jnp.exp(scores - row_top)  13.8 us
    unnamed x107, local copies, waits for them, and re-layouts  13.1 us
    dot_general x4, matrix products, attend_group(): jnp.einsum('hqk,qhd->khd', grad_scores_bf, queries, preferred_element_typ...  13 us
    reshape x4, local copies, waits for them, and re-layouts, per_device(): value_parts.append(grad_v.reshape(-1, col_span))  11.4 us
    reshape x4, local copies, waits for them, and re-layouts, per_device(): key_parts.append(grad_k.reshape(-1, col_span))  10.2 us
  transfers between devices with their start and end apart: 20, of which 1 were waited for; matrix products, arithmetic and copies ran while one was open for 51% of the time, Pallas kernels for 0%

commit v1 on v0

--- a/solution.py
+++ b/solution.py
@@ -206,7 +206,7 @@
                 )
             )
         kernel_rows.append(jnp.stack(kernel_cols, axis=0))
-    grad_kernel = lax.psum(jnp.stack(kernel_rows, axis=0), ("trow", "tcol"))
+    grad_kernel = lax.psum(lax.psum(jnp.stack(kernel_rows, axis=0), "trow"), "tcol")
     grad_query = query_gradient_total.astype(jnp.bfloat16).reshape(
         tile_rows, tile_column_count, channels
     )

time: 373 us -> 451 us (1.21)
  the two profiles are of different devices: /device:TPU:1 before, /device:TPU:129 now
where the time goes in v1:
time: 451 us; the launch traced here: 444 us
  blocking collectives  163 us (36%)
  local copies, waits for them, and re-layouts  108 us (24%)
  starting transfers between devices  68.2 us (15%)
  matrix products  60.8 us (13%)
  other arithmetic  26.8 us (6%)
  between operations  15.3 us (3%)
    psum x1, blocking collectives, per_device(): lax.psum(jnp.stack(kernel_rows, axis=0), 'trow')  114 us
    psum x1, blocking collectives, per_device(): lax.psum(lax.psum(jnp.stack(kernel_rows, axis=0), 'trow'), 'tcol')  49.9 us
    ppermute x8, starting transfers between devices, from_behind(): return lax.ppermute(shard, axis, pairs)  30.1 us
    ppermute x4, starting transfers between devices, with_halo(): lax.ppermute(lax.slice_in_dim(block, 0, width, axis=dim), axis, backward)  16.7 us
    sub x4, matrix products, attend_group(): raised = jnp.exp(scores - row_top)  13.8 us
    unnamed x107, local copies, waits for them, and re-layouts  13.1 us
    dot_general x4, matrix products, attend_group(): jnp.einsum('hqk,qhd->khd', grad_scores_bf, queries, preferred_element_typ...  13 us
    reshape x4, local copies, waits for them, and re-layouts, per_device(): value_parts.append(grad_v.reshape(-1, col_span))  11.4 us
  transfers between devices with their start and end apart: 20, of which 1 were waited for; matrix products, arithmetic and copies ran while one was open for 42% of the time, Pallas kernels for 0%

profile of v1, /device:TPU:129, one launch (start us, length us, event | category | flops | bytes accessed | tf_op | source)
XLA Modules:
  0.0 444.5 jit_solution(10878431707300282132)
XLA Ops:
  8.0 3.9 collective-permute-start.1
  14.9 2.5 collective-permute-start.2
  17.4 6.1 %collective-permute-start.3 = (bf16[1,64,1152]{2,1,0:T(8,128)(2,1)S(1)}, bf16[1,64,1152]{2,1,0:T(8,128)(2,1)S(1)}, u32[]{:S(2)}, u32[]{:S(2)}) collective-permute-start(bf16[1,64,1152]{2,1,0:T(8,128)(2,1)S(1)} %get-tuple-element.54), channel_id=1, source_target_pairs={{8,0},{16,8},{24,16},{32,24},{40,32},{48,40},{56,48},{64,56},{72,6... | collective-permute-start | bytes 442376 | tf_op jit(solution)/shard_map/ppermute | solution.py:21
  28.3 3.7 collective-permute-start.5
  32.0 3.1 collective-permute-start.4
  42.6 5.1 %collective-permute-start.7 = (bf16[128,1152]{1,0:T(8,128)(2,1)}, bf16[128,1152]{1,0:T(8,128)(2,1)}, u32[]{:S(2)}, u32[]{:S(2)}) collective-permute-start(bf16[128,1152]{1,0:T(8,128)(2,1)} %bitcast.12), channel_id=1, source_target_pairs={{8,0},{16,8},{24,16},{32,24},{40,32},{48,40},{56,48},{64,56},{72,6... | collective-permute-start | bytes 884744 | tf_op jit(solution)/shard_map/ppermute | solution.py:29
  49.7 2.7 gather_fusion.1
  53.7 3.0 fusion.101
  59.0 4.0 fusion.108
  63.1 2.7 fusion.109
  73.5 3.0 copy.87
  81.6 2.7 copy.88
  84.4 3.6 fusion.107
  93.1 2.8 copy.89
  96.0 3.5 fusion.106
  104.6 2.8 copy.90
  107.4 8.9 %concatenate.51 = f32[1280,1152]{1,0:T(8,128)} concatenate(f32[1280,288]{1,0:T(8,128)} %copy.87, f32[1280,288]{1,0:T(8,128)} %copy.88, f32[1280,288]{1,0:T(8,128)} %copy.89, f32[1280,288]{1,0:T(8,128)} %copy.90), dimensions={1} | concatenate | bytes 11796480 | tf_op jit(solution)/shard_map/concatenate | solution.py:150
  116.2 3.7 slice.404
  119.9 2.4 fusion.98
  124.2 6.7 %collective-permute-start.10 = (f32[128,1152]{1,0:T(8,128)}, f32[128,1152]{1,0:T(8,128)}, u32[]{:S(2)}, u32[]{:S(2)}) collective-permute-start(f32[128,1152]{1,0:T(8,128)} %get-tuple-element.28), channel_id=1, source_target_pairs={{8,0},{16,8},{24,16},{32,24},{40,32},{48,40},{56,48},{64,56},{72,6... | collective-permute-start | bytes 1769480 | tf_op jit(solution)/shard_map/ppermute | solution.py:29
  132.7 5.8 %scatter_fusion.1 = bf16[8,128,1152]{2,1,0:T(8,128)(2,1)} fusion(bf16[8,128,1152]{2,1,0:T(8,128)(2,1)} %broadcast.125.clone.1, s32[7]{0:T(128)S(1)} %copy-done.44, bf16[7,128,1152]{2,1,0:T(8,128)(2,1)} %bitcast.233), kind=kCustom, calls=%fused_computation.4 | custom fusion | bytes 6193180 | tf_op jit(solution)/shard_map/scatter | solution.py:171
  138.5 4.9 %all-to-all-start.1 = ((bf16[8,128,1152]{2,1,0:T(8,128)(2,1)}), bf16[8,128,1152]{2,1,0:T(8,128)(2,1)}, u32[]{:S(2)}, u32[]{:S(2)}) async-start(bf16[8,128,1152]{2,1,0:T(8,128)(2,1)} %scatter_fusion.1), calls=%async_computation.1 | async-start | bytes 4718592 | tf_op jit(solution)/shard_map/all_to_all | solution.py:174
  143.4 3.9 gather_fusion.2
  149.4 3.6 fusion.100
  156.2 2.5 fusion.28
  164.1 2.5 fusion.29
  172.0 2.5 fusion.30
  178.6 2.5 fusion.31
  183.7 6.4 %pad_maximum_fusion.2 = bf16[2,64,1152]{1,0,2:T(2,128)(2,1)S(1)} fusion(bf16[2,64,288]{1,0,2:T(2,128)(2,1)S(1)} %concatenate.48, bf16[2,64,288]{1,0,2:T(2,128)(2,1)S(1)} %concatenate.47, bf16[2,64,288]{1,0,2:T(2,128)(2,1)} %concatenate.46, bf16[2,64,288]{1,0,2:T(2,128)(2,1)} %concatenate.45), kind=kLoop, calls=%fused_computation.135 | loop fusion | flops 442368 | bytes 589824 | tf_op jit(solution)/shard_map/concatenate | solution.py:148
  191.5 2.9 convolution_multiply_fusion.7
  196.3 3.4 convolution_multiply_fusion.6
  199.6 2.8 copy.80
  202.4 3.3 convolution_multiply_fusion.5
  205.8 2.8 copy.81
  208.6 3.4 convolution_multiply_fusion.4
  211.9 2.7 copy.82
  214.7 8.5 %concatenate.50 = f32[1280,1152]{1,0:T(8,128)} concatenate(f32[1280,288]{1,0:T(8,128)S(1)} %copy.79, f32[1280,288]{1,0:T(8,128)} %copy.80, f32[1280,288]{1,0:T(8,128)} %copy.81, f32[1280,288]{1,0:T(8,128)} %copy.82), dimensions={1} | concatenate | bytes 11796480 | tf_op jit(solution)/shard_map/concatenate | solution.py:149
  223.2 2.4 slice.405
  225.6 2.3 fusion.99
  229.9 6.7 %collective-permute-start.8 = (f32[128,1152]{1,0:T(8,128)}, f32[128,1152]{1,0:T(8,128)}, u32[]{:S(2)}, u32[]{:S(2)}) collective-permute-start(f32[128,1152]{1,0:T(8,128)} %get-tuple-element.30), channel_id=1, source_target_pairs={{8,0},{16,8},{24,16},{32,24},{40,32},{48,40},{56,48},{64,56},{72,6... | collective-permute-start | bytes 1769480 | tf_op jit(solution)/shard_map/ppermute | solution.py:29
  238.4 5.1 %scatter_fusion = bf16[8,128,1152]{2,1,0:T(8,128)(2,1)} fusion(bf16[8,128,1152]{2,1,0:T(8,128)(2,1)} %broadcast.125.clone, s32[7]{0:T(128)S(1)} %copy-done.45, bf16[7,128,1152]{2,1,0:T(8,128)(2,1)S(1)} %bitcast.232), kind=kCustom, calls=%fused_computation.3 | custom fusion | bytes 6193180 | tf_op jit(solution)/shard_map/scatter | solution.py:170
  243.5 5.5 %all-to-all-start = ((bf16[8,128,1152]{2,1,0:T(8,128)(2,1)}), bf16[8,128,1152]{2,1,0:T(8,128)(2,1)}, u32[]{:S(2)}, u32[]{:S(2)}) async-start(bf16[8,128,1152]{2,1,0:T(8,128)(2,1)} %scatter_fusion), calls=%async_computation | async-start | bytes 4718592 | tf_op jit(solution)/shard_map/all_to_all | solution.py:173
  248.9 3.3 fusion.32
  255.7 3.4 collective-permute-start.12
  259.9 113.6 %psum.14 = f32[3,3,1152]{2,1,0:T(4,128)S(1)} all-reduce(f32[3,3,1152]{2,1,0:T(4,128)S(1)} %pad_maximum_fusion.3), channel_id=1, replica_groups=mesh['trow'=32,'tcol'=8] {'trow'}, use_global_device_ids=true, to_apply=%region_23.24 | all-reduce | flops 10368 | bytes 82944 | tf_op jit(solution)/shard_map/psum | solution.py:209
  373.4 49.9 %psum.15 = f32[3,3,1152]{2,1,0:T(4,128)} all-reduce(f32[3,3,1152]{2,1,0:T(4,128)S(1)} %psum.14), channel_id=1, replica_groups=mesh['trow'=32,'tcol'=8] {'tcol'}, use_global_device_ids=true, to_apply=%region_24.25 | all-reduce | flops 10368 | bytes 82944 | tf_op jit(solution)/shard_map/psum | solution.py:209
  423.3 5.0 %collective-permute-start.15 = (bf16[4,1,1152]{2,1,0:T(2,128)(2,1)S(1)}, bf16[4,1,1152]{2,1,0:T(2,128)(2,1)S(1)}, u32[]{:S(2)}, u32[]{:S(2)}) collective-permute-start(bf16[4,1,1152]{2,1,0:T(2,128)(2,1)S(1)} %get-tuple-element.41), channel_id=1, source_target_pairs={{1,0},{2,1},{3,2},{4,3},{5,4},{6,5},{7,6},{9,8},{10,9},{11,10},{12... | collective-permute-start | bytes 27656 | tf_op jit(solution)/shard_map/ppermute | solution.py:21
  430.3 3.3 fusion.34
  (210 shorter events, 87.2 us)
Async XLA Ops:
  7.2 21.0 %copy-start.14 = (bf16[2,64,1152]{2,1,0:T(8,128)(2,1)S(1)}, bf16[2,64,1152]{2,1,0:T(8,128)(2,1)}, u32[]{:S(2)}) copy-start(bf16[2,64,1152]{2,1,0:T(8,128)(2,1)} %param.10) | copy-start | bytes 884740
  7.2 19.0 %copy-start.17 = (bf16[2,64,1152]{2,1,0:T(8,128)(2,1)S(1)}, bf16[2,64,1152]{2,1,0:T(8,128)(2,1)}, u32[]{:S(2)}) copy-start(bf16[2,64,1152]{2,1,0:T(8,128)(2,1)} %param.7) | copy-start | bytes 884740
  7.2 19.8 %copy-start.41 = (f32[3,3,1152]{2,1,0:T(4,128)S(1)}, f32[3,3,1152]{2,1,0:T(4,128)}, u32[]{:S(2)}) copy-start(f32[3,3,1152]{2,1,0:T(4,128)} %param.11) | copy-start | bytes 124420
  7.2 42.5 %all-gather.3.cloned.1.call-start = ((), (), s32[]{:S(2)}) async-start(), calls=%async_computation.2 | async-start | bytes 2654208 | tf_op jit(solution)/shard_map/all_gather | solution.py:108
  7.9 135.5 %all-gather.5.cloned.1.call-start = ((), (), s32[]{:S(2)}) async-start(), calls=%async_computation.3 | async-start | bytes 2654208 | tf_op jit(solution)/shard_map/all_gather | solution.py:109
  8.0 44.4 %collective-permute-start.1 = (bf16[128,1152]{1,0:T(8,128)(2,1)}, bf16[128,1152]{1,0:T(8,128)(2,1)}, u32[]{:S(2)}, u32[]{:S(2)}) collective-permute-start(bf16[128,1152]{1,0:T(8,128)(2,1)} %bitcast.266), channel_id=1, source_target_pairs={{8,0},{16,8},{24,16},{32,24},{40,32},{48,40},{56,48},{64,56},{72,6... | collective-permute-start | bytes 884744 | tf_op jit(solution)/shard_map/ppermute | solution.py:29
  11.9 40.5 %collective-permute-start = (bf16[128,1152]{1,0:T(8,128)(2,1)}, bf16[128,1152]{1,0:T(8,128)(2,1)}, u32[]{:S(2)}, u32[]{:S(2)}) collective-permute-start(bf16[128,1152]{1,0:T(8,128)(2,1)} %bitcast.267), channel_id=1, source_target_pairs={{0,8},{8,16},{16,24},{24,32},{32,40},{40,48},{48,56},{56,64},{64,7... | collective-permute-start | bytes 884744 | tf_op jit(solution)/shard_map/ppermute | solution.py:29
  14.9 13.3 %collective-permute-start.2 = (bf16[1,64,1152]{2,1,0:T(8,128)(2,1)S(1)}, bf16[1,64,1152]{2,1,0:T(8,128)(2,1)S(1)}, u32[]{:S(2)}, u32[]{:S(2)}) collective-permute-start(bf16[1,64,1152]{2,1,0:T(8,128)(2,1)S(1)} %get-tuple-element.55), channel_id=1, source_target_pairs={{0,8},{8,16},{16,24},{24,32},{32,40},{40,48},{48,56},{56,64},{64,7... | collective-permute-start | bytes 442376 | tf_op jit(solution)/shard_map/ppermute | solution.py:18
  17.4 10.8 %collective-permute-start.3 = (bf16[1,64,1152]{2,1,0:T(8,128)(2,1)S(1)}, bf16[1,64,1152]{2,1,0:T(8,128)(2,1)S(1)}, u32[]{:S(2)}, u32[]{:S(2)}) collective-permute-start(bf16[1,64,1152]{2,1,0:T(8,128)(2,1)S(1)} %get-tuple-element.54), channel_id=1, source_target_pairs={{8,0},{16,8},{24,16},{32,24},{40,32},{48,40},{56,48},{64,56},{72,6... | collective-permute-start | bytes 442376 | tf_op jit(solution)/shard_map/ppermute | solution.py:21
  24.2 16.2 %copy-start.46 = (s32[1,8,8]{2,1,0:T(8,128)S(1)}, s32[1,8,8]{2,1,0:T(8,128)}, u32[]{:S(2)}) copy-start(s32[1,8,8]{2,1,0:T(8,128)} %param.13) | copy-start | bytes 772
  27.0 14.4 %copy-start.18 = (bf16[2,64,1152]{2,1,0:T(8,128)(2,1)S(1)}, bf16[2,64,1152]{2,1,0:T(8,128)(2,1)}, u32[]{:S(2)}) copy-start(bf16[2,64,1152]{2,1,0:T(8,128)(2,1)} %param.9) | copy-start | bytes 884740
  27.1 15.5 %copy-start.27 = (f32[1152]{0:T(1024)}, f32[1152]{0:T(1024)S(1)}, u32[]{:S(2)}) copy-start(f32[1152]{0:T(1024)S(1)} %get-tuple-element.21) | copy-start | bytes 13828
  27.1 15.5 %copy-start.29 = (f32[1152]{0:T(1024)}, f32[1152]{0:T(1024)S(1)}, u32[]{:S(2)}) copy-start(f32[1152]{0:T(1024)S(1)} %get-tuple-element.22) | copy-start | bytes 13828
  27.1 15.5 %copy-start.31 = (f32[1152]{0:T(1024)}, f32[1152]{0:T(1024)S(1)}, u32[]{:S(2)}) copy-start(f32[1152]{0:T(1024)S(1)} %get-tuple-element.23) | copy-start | bytes 13828
  27.1 15.5 %copy-start.33 = (f32[1152]{0:T(1024)}, f32[1152]{0:T(1024)S(1)}, u32[]{:S(2)}) copy-start(f32[1152]{0:T(1024)S(1)} %get-tuple-element.24) | copy-start | bytes 13828
  27.1 15.5 %copy-start.35 = (f32[1152]{0:T(1024)}, f32[1152]{0:T(1024)S(1)}, u32[]{:S(2)}) copy-start(f32[1152]{0:T(1024)S(1)} %get-tuple-element.25) | copy-start | bytes 13828
  27.1 15.5 %copy-start.37 = (f32[1152]{0:T(1024)}, f32[1152]{0:T(1024)S(1)}, u32[]{:S(2)}) copy-start(f32[1152]{0:T(1024)S(1)} %get-tuple-element.26) | copy-start | bytes 13828
  27.1 15.5 %copy-start.39 = (f32[1152]{0:T(1024)}, f32[1152]{0:T(1024)S(1)}, u32[]{:S(2)}) copy-start(f32[1152]{0:T(1024)S(1)} %get-tuple-element.27) | copy-start | bytes 13828
  28.3 12.9 %collective-permute-start.5 = (bf16[4,1,1152]{2,1,0:T(2,128)(2,1)S(1)}, bf16[4,1,1152]{2,1,0:T(2,128)(2,1)S(1)}, u32[]{:S(2)}, u32[]{:S(2)}) collective-permute-start(bf16[4,1,1152]{2,1,0:T(2,128)(2,1)S(1)} %get-tuple-element.43), channel_id=1, source_target_pairs={{1,0},{2,1},{3,2},{4,3},{5,4},{6,5},{7,6},{9,8},{10,9},{11,10},{12... | collective-permute-start | bytes 27656 | tf_op jit(solution)/shard_map/ppermute | solution.py:21
  32.0 9.2 %collective-permute-start.4 = (bf16[4,1,1152]{2,1,0:T(2,128)(2,1)S(1)}, bf16[4,1,1152]{2,1,0:T(2,128)(2,1)S(1)}, u32[]{:S(2)}, u32[]{:S(2)}) collective-permute-start(bf16[4,1,1152]{2,1,0:T(2,128)(2,1)S(1)} %get-tuple-element.42), channel_id=1, source_target_pairs={{0,1},{1,2},{2,3},{3,4},{4,5},{5,6},{6,7},{8,9},{9,10},{10,11},{11... | collective-permute-start | bytes 27656 | tf_op jit(solution)/shard_map/ppermute | solution.py:18
  42.6 104.8 %collective-permute-start.7 = (bf16[128,1152]{1,0:T(8,128)(2,1)}, bf16[128,1152]{1,0:T(8,128)(2,1)}, u32[]{:S(2)}, u32[]{:S(2)}) collective-permute-start(bf16[128,1152]{1,0:T(8,128)(2,1)} %bitcast.12), channel_id=1, source_target_pairs={{8,0},{16,8},{24,16},{32,24},{40,32},{48,40},{56,48},{64,56},{72,6... | collective-permute-start | bytes 884744 | tf_op jit(solution)/shard_map/ppermute | solution.py:29
  47.7 99.7 %collective-permute-start.6 = (bf16[128,1152]{1,0:T(8,128)(2,1)}, bf16[128,1152]{1,0:T(8,128)(2,1)}, u32[]{:S(2)}, u32[]{:S(2)}) collective-permute-start(bf16[128,1152]{1,0:T(8,128)(2,1)} %bitcast.12), channel_id=1, source_target_pairs={{0,8},{8,16},{16,24},{24,32},{32,40},{40,48},{48,56},{56,64},{64,7... | collective-permute-start | bytes 884744 | tf_op jit(solution)/shard_map/ppermute | solution.py:29
  59.0 4.1 copy-start.7
  59.0 4.0 copy-start.26
  73.5 10.9 %copy-start.10 = (bf16[1280,288]{0,1:T(8,128)(2,1)}, bf16[1280,288]{0,1:T(8,128)(2,1)S(1)}, u32[]{:S(2)}) copy-start(bf16[1280,288]{0,1:T(8,128)(2,1)S(1)} %copy.63) | copy-start | bytes 2211844
  88.0 3.1 copy-start.15
  93.1 2.9 copy-start.12
  99.5 3.0 copy-start.16
  119.9 12.7 %copy-start.44 = (s32[7]{0:T(128)S(1)}, s32[7]{0:T(128)}, u32[]{:S(2)}) copy-start(s32[7]{0:T(128)} %copy-done.43) | copy-start | bytes 88
  122.3 129.9 %collective-permute-start.11 = (f32[128,1152]{1,0:T(8,128)}, f32[128,1152]{1,0:T(8,128)}, u32[]{:S(2)}, u32[]{:S(2)}) collective-permute-start(f32[128,1152]{1,0:T(8,128)} %get-tuple-element.29), channel_id=1, source_target_pairs={{0,8},{8,16},{16,24},{24,32},{32,40},{40,48},{48,56},{56,64},{64,7... | collective-permute-start | bytes 1769480 | tf_op jit(solution)/shard_map/ppermute | solution.py:29
  124.2 128.0 %collective-permute-start.10 = (f32[128,1152]{1,0:T(8,128)}, f32[128,1152]{1,0:T(8,128)}, u32[]{:S(2)}, u32[]{:S(2)}) collective-permute-start(f32[128,1152]{1,0:T(8,128)} %get-tuple-element.28), channel_id=1, source_target_pairs={{8,0},{16,8},{24,16},{32,24},{40,32},{48,40},{56,48},{64,56},{72,6... | collective-permute-start | bytes 1769480 | tf_op jit(solution)/shard_map/ppermute | solution.py:29
  138.5 105.0 %all-to-all-start.1 = ((bf16[8,128,1152]{2,1,0:T(8,128)(2,1)}), bf16[8,128,1152]{2,1,0:T(8,128)(2,1)}, u32[]{:S(2)}, u32[]{:S(2)}) async-start(bf16[8,128,1152]{2,1,0:T(8,128)(2,1)} %scatter_fusion.1), calls=%async_computation.1 | async-start | bytes 4718592 | tf_op jit(solution)/shard_map/all_to_all | solution.py:174
  156.2 3.6 copy-start.13
  164.1 3.7 copy-start.11
  172.0 3.6 copy-start.9
  178.6 3.0 copy-start.19
  199.6 2.8 copy-start.23
  205.8 2.8 copy-start.22
  225.6 12.7 %copy-start.45 = (s32[7]{0:T(128)S(1)}, s32[7]{0:T(128)}, u32[]{:S(2)}) copy-start(s32[7]{0:T(128)} %copy-done.43) | copy-start | bytes 88
  228.0 205.7 %collective-permute-start.9 = (f32[128,1152]{1,0:T(8,128)}, f32[128,1152]{1,0:T(8,128)}, u32[]{:S(2)}, u32[]{:S(2)}) collective-permute-start(f32[128,1152]{1,0:T(8,128)} %get-tuple-element.31), channel_id=1, source_target_pairs={{0,8},{8,16},{16,24},{24,32},{32,40},{40,48},{48,56},{56,64},{64,7... | collective-permute-start | bytes 1769480 | tf_op jit(solution)/shard_map/ppermute | solution.py:29
  229.9 203.8 %collective-permute-start.8 = (f32[128,1152]{1,0:T(8,128)}, f32[128,1152]{1,0:T(8,128)}, u32[]{:S(2)}, u32[]{:S(2)}) collective-permute-start(f32[128,1152]{1,0:T(8,128)} %get-tuple-element.30), channel_id=1, source_target_pairs={{8,0},{16,8},{24,16},{32,24},{40,32},{48,40},{56,48},{64,56},{72,6... | collective-permute-start | bytes 1769480 | tf_op jit(solution)/shard_map/ppermute | solution.py:29
  243.5 5.5 %copy-start.42 = (pred[8]{0:T(512)(128)(4,1)S(1)}, pred[8]{0:T(512)(128)(4,1)}, u32[]{:S(2)}) copy-start(pred[8]{0:T(512)(128)(4,1)} %fusion.80) | copy-start | bytes 28
  243.5 186.8 %all-to-all-start = ((bf16[8,128,1152]{2,1,0:T(8,128)(2,1)}), bf16[8,128,1152]{2,1,0:T(8,128)(2,1)}, u32[]{:S(2)}, u32[]{:S(2)}) async-start(bf16[8,128,1152]{2,1,0:T(8,128)(2,1)} %scatter_fusion), calls=%async_computation | async-start | bytes 4718592 | tf_op jit(solution)/shard_map/all_to_all | solution.py:173
  253.7 182.2 %copy-start.3 = (bf16[128,1152]{1,0:T(8,128)(2,1)}, bf16[128,1152]{1,0:T(8,128)(2,1)S(1)}, u32[]{:S(2)}) copy-start(bf16[128,1152]{1,0:T(8,128)(2,1)S(1)} %fusion.76) | copy-start | bytes 884740
  253.8 169.5 %collective-permute-start.13 = (bf16[1,64,1152]{2,1,0:T(8,128)(2,1)S(1)}, bf16[1,64,1152]{2,1,0:T(8,128)(2,1)S(1)}, u32[]{:S(2)}, u32[]{:S(2)}) collective-permute-start(bf16[1,64,1152]{2,1,0:T(8,128)(2,1)S(1)} %get-tuple-element.45), channel_id=1, source_target_pairs={{8,0},{16,8},{24,16},{32,24},{40,32},{48,40},{56,48},{64,56},{72,6... | collective-permute-start | bytes 442376 | tf_op jit(solution)/shard_map/ppermute | solution.py:21
  255.7 167.6 %collective-permute-start.12 = (bf16[1,64,1152]{2,1,0:T(8,128)(2,1)S(1)}, bf16[1,64,1152]{2,1,0:T(8,128)(2,1)S(1)}, u32[]{:S(2)}, u32[]{:S(2)}) collective-permute-start(bf16[1,64,1152]{2,1,0:T(8,128)(2,1)S(1)} %get-tuple-element.44), channel_id=1, source_target_pairs={{0,8},{8,16},{16,24},{24,32},{32,40},{40,48},{48,56},{56,64},{64,7... | collective-permute-start | bytes 442376 | tf_op jit(solution)/shard_map/ppermute | solution.py:18
  423.3 12.6 %collective-permute-start.15 = (bf16[4,1,1152]{2,1,0:T(2,128)(2,1)S(1)}, bf16[4,1,1152]{2,1,0:T(2,128)(2,1)S(1)}, u32[]{:S(2)}, u32[]{:S(2)}) collective-permute-start(bf16[4,1,1152]{2,1,0:T(2,128)(2,1)S(1)} %get-tuple-element.41), channel_id=1, source_target_pairs={{1,0},{2,1},{3,2},{4,3},{5,4},{6,5},{7,6},{9,8},{10,9},{11,10},{12... | collective-permute-start | bytes 27656 | tf_op jit(solution)/shard_map/ppermute | solution.py:21
  428.4 7.6 %collective-permute-start.14 = (bf16[4,1,1152]{2,1,0:T(2,128)(2,1)S(1)}, bf16[4,1,1152]{2,1,0:T(2,128)(2,1)S(1)}, u32[]{:S(2)}, u32[]{:S(2)}) collective-permute-start(bf16[4,1,1152]{2,1,0:T(2,128)(2,1)S(1)} %get-tuple-element.40), channel_id=1, source_target_pairs={{0,1},{1,2},{2,3},{3,4},{4,5},{5,6},{6,7},{8,9},{9,10},{10,11},{11... | collective-permute-start | bytes 27656 | tf_op jit(solution)/shard_map/ppermute | solution.py:18
  (20 other events, 36.6 us)
Sparse Core Ops, SparseCore 0:
  9.8 30.0 all-gather.2
  49.8 29.1 all-gather.4
